TPU v7x, 256 devices: a whole 4x4x8 slice. The times are simulated.
256 devices in a mesh: shot: 32 (over y_hi, z, core), rcv: 8 (over x, y_lo).
Axes of the slice: x: 4, y: 4 (y_hi: 2, y_lo: 2; y = y_hi * 2 + y_lo), z: 8, core: 2. Of those that a mesh axis runs over, the one named last changes fastest.
Arguments:
- record: bfloat16 [768, 262144], P('rcv', 'shot'), may hold values from -6 to 6
- shot_fire_samples: int32 [1024], P('shot'), may hold values from 0 to 262143, as said below
Outputs:
- psf_gram: float32 [2, 4, 768, 768], P(None, None, 'rcv', 'shot')
Inputs may be any that keep to these rules, and one draw needn't show every extreme that they name: `shot_fire_samples`: shot s fires at a sample from s * 256 to s * 256 + 255.
All inputs are finite; a program needn't handle non-finite values.
Results may differ from a plain program's by a relative error of at most 0.0025.
Values may be sent and summed in bfloat16 or wider, within the bound.
No kernel may reach another device: no remote copies, remote signals or barrier semaphores. Data moves between devices by JAX's collectives and lax.ppermute only.
A program may use at most 64 MiB of HBM per device.

v0:
```python
import math
import jax
import jax.numpy as jnp
from jax import lax
from jax.sharding import PartitionSpec as P

WIN = 2048
SPACING = 256
freq_bins = (24, 40, 56, 80)


def shifted(block, axis, distance):
    devices = range(lax.axis_size(axis))
    route = [(i - distance, i) for i in devices if i - distance in devices]
    return lax.ppermute(block, axis, route)


def dft_table(window_len):
    lag_index = jnp.arange(window_len, dtype=jnp.int32)
    bin_list = jnp.array(freq_bins, dtype=jnp.int32)
    turn_count = lag_index[:, None] * bin_list[None, :] % window_len
    phase_angle = 2.0 * math.pi / window_len * turn_count.astype(jnp.float32)
    dft_rows = jnp.concatenate([jnp.cos(phase_angle), -jnp.sin(phase_angle)], axis=1) / math.sqrt(
        window_len
    )
    return dft_rows.astype(jnp.bfloat16)


def shifted_tables(jitter, span):
    lag_index = jnp.arange(span, dtype=jnp.int32)[None, :] - jitter[:, None]
    inside = (lag_index >= 0) & (lag_index < WIN)
    clipped = jnp.clip(lag_index, 0, WIN - 1)
    bin_list = jnp.array(freq_bins, dtype=jnp.int32)
    turn_count = clipped[:, None, :] * bin_list[None, :, None] % WIN
    phase_angle = 2.0 * math.pi / WIN * turn_count.astype(jnp.float32)
    table = jnp.concatenate([jnp.cos(phase_angle), -jnp.sin(phase_angle)], axis=1) / math.sqrt(WIN)
    table = jnp.where(inside[:, None, :], table, 0.0)
    return table.astype(jnp.bfloat16)


def local_spectra(extended, sample_offsets, dft_rows):
    count_of_shots = sample_offsets.shape[0]
    reach_blocks = WIN // SPACING + 1
    jitter = sample_offsets - jnp.arange(count_of_shots, dtype=jnp.int32) * SPACING
    tables = shifted_tables(jitter, reach_blocks * SPACING)
    tables = tables.reshape(count_of_shots, dft_rows.shape[1], reach_blocks, SPACING)
    blocks = extended.reshape(extended.shape[0], extended.shape[1] // SPACING, SPACING)
    total = jnp.zeros((count_of_shots, dft_rows.shape[1], extended.shape[0]), jnp.float32)
    for offset in range(reach_blocks):
        record_part = blocks[:, offset : offset + count_of_shots, :]
        total = total + jnp.einsum(
            "rsu,scu->scr", record_part, tables[:, :, offset, :], preferred_element_type=jnp.float32
        )
    return total


def gram_terms(left, right):
    nfreq = len(freq_bins)
    left_re = left[:, :nfreq, :]
    left_im = left[:, nfreq:, :]
    right_re = right[:, :nfreq, :]
    right_im = right[:, nfreq:, :]
    gram_real = jnp.einsum("sfr,sfq->frq", left_re, right_re, preferred_element_type=jnp.float32)
    gram_real = gram_real + jnp.einsum(
        "sfr,sfq->frq", left_im, right_im, preferred_element_type=jnp.float32
    )
    gram_imag = jnp.einsum("sfr,sfq->frq", left_re, right_im, preferred_element_type=jnp.float32)
    gram_imag = gram_imag - jnp.einsum(
        "sfr,sfq->frq", left_im, right_re, preferred_element_type=jnp.float32
    )
    return jnp.stack([gram_real, gram_imag], axis=0)


def per_device(record, shot_fire_samples):
    trace_segment_length = record.shape[1]
    count_of_shots = shot_fire_samples.shape[0]
    dft_rows = dft_table(WIN)
    sample_offsets = shot_fire_samples - lax.axis_index("shot") * trace_segment_length
    head_rows = record[:, :WIN]
    rim_rows = shifted(head_rows, "shot", -1)
    extended = jnp.concatenate([record, rim_rows], axis=1)
    trace_spectra = local_spectra(extended, sample_offsets, dft_rows)
    trace_spectra = trace_spectra.astype(jnp.bfloat16)
    all_receivers = lax.all_gather(trace_spectra, "rcv", axis=2, tiled=True)
    total_shots = count_of_shots * lax.axis_size("shot")
    partial_gram = gram_terms(trace_spectra, all_receivers)
    result = lax.psum_scatter(partial_gram, "shot", scatter_dimension=3, tiled=True)
    return result / total_shots


def solution(mesh):
    return jax.shard_map(
        per_device,
        mesh=mesh,
        in_specs=(P("rcv", "shot"), P("shot")),
        out_specs=P(None, None, "rcv", "shot"),
        check_vma=False,
    )
```

profile of v0, /device:TPU:1, one launch (start us, length us, event | category | flops | bytes accessed | tf_op | source)
XLA Modules:
  0.0 363.7 jit_solution(5917377322379942619)
XLA Ops:
  6.5 0.0 all-reduce.3.cloned.1.call-start
  6.5 1.0 slice.70
  7.6 5.1 %collective-permute-start = (bf16[96,2048]{1,0:T(8,128)(2,1)S(1)}, bf16[96,2048]{1,0:T(8,128)(2,1)S(1)}, u32[]{:S(2)}, u32[]{:S(2)}) collective-permute-start(bf16[96,2048]{1,0:T(8,128)(2,1)S(1)} %slice.70), channel_id=1, source_target_pairs={{8,0},{16,8},{24,16},{32,24},{40,32},{48,40},{56,48},{64,56},{72,6... | collective-permute-start | bytes 1179656 | tf_op jit(solution)/shard_map/ppermute | solution.py:15
  12.7 0.7 multiply_subtract_fusion
  13.4 0.1 subtract_clamp_fusion
  13.5 10.4 %fusion.52 = (f32[32,4,9,256]{3,1,0,2:T(4,128)S(1)}, f32[32,4,9,256]{3,1,0,2:T(4,128)S(1)}) fusion(s32[4]{0:T(128)} %constant.43.clone, s32[32,9,256]{2,0,1:T(8,128)S(1)} %subtract_clamp_fusion), kind=kLoop, calls=%fused_computation.45 | loop fusion | flops 4423680 | bytes 2654224 | tf_op jit(solution)/shard_map/cos | solution.py:36
  23.9 0.1 fusion.53
  24.1 0.0 copy-start
  24.1 0.8 fusion.1
  24.9 0.0 collective-permute-done
  24.9 0.5 copy-done
  25.5 0.1 pad_maximum_fusion.1
  25.6 0.5 copy.78
  26.1 3.3 fusion.60
  29.5 0.9 fusion.16
  30.4 0.9 fusion.14
  31.3 0.9 fusion.12
  32.3 0.9 fusion.8
  33.2 0.9 fusion.6
  34.2 0.9 fusion.2
  35.1 1.0 fusion.31
  36.1 1.0 fusion.40
  37.1 1.0 fusion.49
  38.0 0.2 copy.58
  38.2 32.1 %all_gather.3 = bf16[32,8,768]{0,1,2:T(8,128)(2,1)S(1)} all-gather(bf16[32,8,96]{0,1,2:T(8,128)(2,1)S(1)} %copy.58), channel_id=1, replica_groups=mesh['shot'=32,'rcv'=8] {'rcv'}, dimensions={2}, use_global_device_ids=true | all-gather | bytes 442368 | tf_op jit(solution)/shard_map/all_gather | solution.py:84
  70.4 0.5 fusion.61
  70.9 0.5 copy.76
  71.4 0.5 copy.77
  71.9 0.4 fusion.58
  72.3 0.4 fusion.56
  72.6 0.4 fusion.21
  73.0 0.3 fusion.20
  73.3 0.2 pad_maximum_fusion
  73.5 2.8 copy.65
  76.3 0.0 copy-start.1
  76.3 0.0 all-reduce.3.cloned.1.call-update
  76.4 0.6 copy-done.1
  77.0 0.6 dynamic-slice
  78.2 277.0 %all-reduce.3.cloned.1.call-done = f32[2,4,96,768]{2,1,0,3:T(4,128)} async-done(((f32[2,4,96,768]{2,1,0,3:T(4,128)}), f32[2,4,96,768]{2,1,0,3:T(4,128)}) %all-reduce.3.cloned.1.call-update) | async-done | bytes 2359312
  355.3 0.9 constant_dynamic-slice_fusion
  356.2 0.7 copy_multiply_fusion
  (2 shorter events, 0.0 us)
Async XLA Ops:
  6.5 348.7 %all-reduce.3.cloned.1.call-start = ((), (), s32[]{:S(2)}) async-start(), calls=%async_computation | async-start | bytes 6291456
  7.6 17.4 %collective-permute-start = (bf16[96,2048]{1,0:T(8,128)(2,1)S(1)}, bf16[96,2048]{1,0:T(8,128)(2,1)S(1)}, u32[]{:S(2)}, u32[]{:S(2)}) collective-permute-start(bf16[96,2048]{1,0:T(8,128)(2,1)S(1)} %slice.70), channel_id=1, source_target_pairs={{8,0},{16,8},{24,16},{32,24},{40,32},{48,40},{56,48},{64,56},{72,6... | collective-permute-start | bytes 1179656 | tf_op jit(solution)/shard_map/ppermute | solution.py:15
  24.1 1.4 copy-start
  76.3 0.7 copy-start.1
Sparse Core Ops, SparseCore 0:
  76.5 278.7 all-reduce.2
where the time goes:
time: 364 us
  waiting for transfers between devices  277 us (76%)
  blocking collectives  32.1 us (9%)
  between operations  14.2 us (4%)
  other arithmetic  13.1 us (4%)
  local copies, waits for them, and re-layouts  12 us (3%)
  matrix products  9.99 us (3%)
  starting transfers between devices  5.15 us (1%)
    unnamed x2, waiting for transfers between devices  277 us
    all_gather x1, blocking collectives, per_device(): all_receivers = lax.all_gather(trace_spectra, 'rcv', axis=2, tiled=True)  32.1 us
    cos x1, other arithmetic, shifted_tables(): jnp.cos(phase_angle)  10.4 us
    dot_general x9, matrix products, local_spectra(): jnp.einsum('rsu,scu->scr', record_part, tables[:, :, offset, :], preferre...  8.57 us
  transfers between devices with their start and end apart: 2, of which 1 were waited for; matrix products, arithmetic and copies ran while one was open for 4% of the time, Pallas kernels for 0%

commit v1 on v0

--- a/solution.py
+++ b/solution.py
@@ -81,7 +81,10 @@
     extended = jnp.concatenate([record, rim_rows], axis=1)
     trace_spectra = local_spectra(extended, sample_offsets, dft_rows)
     trace_spectra = trace_spectra.astype(jnp.bfloat16)
-    all_receivers = lax.all_gather(trace_spectra, "rcv", axis=2, tiled=True)
+    size = lax.axis_size("rcv")
+    pieces = jnp.stack([trace_spectra for _ in range(size)])
+    pieces = lax.all_to_all(pieces, "rcv", split_axis=0, concat_axis=0)
+    all_receivers = jnp.concatenate(pieces, axis=2)
     total_shots = count_of_shots * lax.axis_size("shot")
     partial_gram = gram_terms(trace_spectra, all_receivers)
     result = lax.psum_scatter(partial_gram, "shot", scatter_dimension=3, tiled=True)

time: 364 us -> 342 us (0.940)
  blocking collectives: 32.1 us -> 0 us
  waiting for transfers between devices: 277 us -> 284 us
    all_gather x1 -> x0, blocking collectives: 32.1 us -> none  [per_device(): all_receivers = lax.all_gather(trace_spectra, 'rcv', axis=2, tiled=True)]
    all_to_all x0 -> x1, waiting for transfers between devices: none -> 10.3 us  [per_device(): pieces = lax.all_to_all(pieces, 'rcv', split_axis=0, concat_axis=0)]
  transfers between devices with their start and end apart: 2 -> 3, of which waited for: 1 -> 2; matrix products, arithmetic and copies ran while one was open for 4% -> 4% of each run, Pallas kernels for 0% -> 0%
where the time goes in v1:
time: 342 us
  waiting for transfers between devices  284 us (83%)
  between operations  14.2 us (4%)
  other arithmetic  13.1 us (4%)
  local copies, waits for them, and re-layouts  12 us (4%)
  matrix products  9.98 us (3%)
  starting transfers between devices  8.68 us (3%)
    unnamed x2, waiting for transfers between devices  274 us
    cos x1, other arithmetic, shifted_tables(): jnp.cos(phase_angle)  10.4 us
    all_to_all x1, waiting for transfers between devices, per_device(): pieces = lax.all_to_all(pieces, 'rcv', split_axis=0, concat_axis=0)  10.3 us
    dot_general x9, matrix products, local_spectra(): jnp.einsum('rsu,scu->scr', record_part, tables[:, :, offset, :], preferre...  8.57 us
  transfers between devices with their start and end apart: 3, of which 2 were waited for; matrix products, arithmetic and copies ran while one was open for 4% of the time, Pallas kernels for 0%

profile of v1, /device:TPU:1, one launch (start us, length us, event | category | flops | bytes accessed | tf_op | source)
XLA Modules:
  0.0 341.8 jit_solution(15764698341918855879)
XLA Ops:
  6.5 1.0 slice.70
  7.6 5.1 %collective-permute-start = (bf16[96,2048]{1,0:T(8,128)(2,1)S(1)}, bf16[96,2048]{1,0:T(8,128)(2,1)S(1)}, u32[]{:S(2)}, u32[]{:S(2)}) collective-permute-start(bf16[96,2048]{1,0:T(8,128)(2,1)S(1)} %slice.70), channel_id=1, source_target_pairs={{8,0},{16,8},{24,16},{32,24},{40,32},{48,40},{56,48},{64,56},{72,6... | collective-permute-start | bytes 1179656 | tf_op jit(solution)/shard_map/ppermute | solution.py:15
  12.7 0.7 multiply_subtract_fusion
  13.4 0.1 subtract_clamp_fusion
  13.5 10.4 %fusion.52 = (f32[32,4,9,256]{3,1,0,2:T(4,128)S(1)}, f32[32,4,9,256]{3,1,0,2:T(4,128)S(1)}) fusion(s32[4]{0:T(128)} %constant.43.clone, s32[32,9,256]{2,0,1:T(8,128)S(1)} %subtract_clamp_fusion), kind=kLoop, calls=%fused_computation.45 | loop fusion | flops 4423680 | bytes 2654224 | tf_op jit(solution)/shard_map/cos | solution.py:36
  23.9 0.1 fusion.53
  24.1 0.0 copy-start
  24.1 0.8 fusion.1
  24.9 0.0 collective-permute-done
  24.9 0.5 copy-done
  25.5 0.1 pad_maximum_fusion.1
  25.6 0.5 copy.68
  26.1 3.3 fusion.64
  29.4 0.9 fusion.16
  30.4 0.9 fusion.14
  31.3 0.9 fusion.12
  32.3 0.9 fusion.8
  33.2 0.9 fusion.6
  34.2 0.9 fusion.2
  35.1 1.0 fusion.31
  36.1 1.0 fusion.40
  37.1 1.0 fusion.49
  38.0 0.9 stack.8
  38.9 3.5 %all-to-all-start = ((bf16[8,32,8,96]{3,1,2,0:T(8,128)(2,1)}), bf16[8,32,8,96]{3,1,2,0:T(8,128)(2,1)S(1)}, u32[]{:S(2)}, u32[]{:S(2)}) async-start(bf16[8,32,8,96]{3,1,2,0:T(8,128)(2,1)} %stack.8), calls=%async_computation | async-start | bytes 1048576 | tf_op jit(solution)/shard_map/all_to_all | solution.py:86
  42.4 0.0 all-reduce.3.cloned.1.call-start
  42.5 10.3 %all-to-all-done = bf16[8,32,8,96]{3,1,2,0:T(8,128)(2,1)S(1)} async-done(((bf16[8,32,8,96]{3,1,2,0:T(8,128)(2,1)}), bf16[8,32,8,96]{3,1,2,0:T(8,128)(2,1)S(1)}, u32[]{:S(2)}, u32[]{:S(2)}) %all-to-all-start) | async-done | bytes 393248 | tf_op jit(solution)/shard_map/all_to_all | solution.py:86
  52.8 0.3 copy.52
  53.1 0.4 reshape.68
  53.5 0.4 fusion.58
  53.9 0.3 fusion.54
  54.2 0.4 fusion.21
  54.6 0.4 fusion.20
  55.0 0.2 pad_maximum_fusion
  55.1 2.8 copy.57
  58.0 0.0 copy-start.1
  58.0 0.0 all-reduce.3.cloned.1.call-update
  58.0 0.6 copy-done.1
  58.6 0.6 dynamic-slice
  59.9 273.5 %all-reduce.3.cloned.1.call-done = f32[2,4,96,768]{2,1,0,3:T(4,128)} async-done(((f32[2,4,96,768]{2,1,0,3:T(4,128)}), f32[2,4,96,768]{2,1,0,3:T(4,128)}) %all-reduce.3.cloned.1.call-update) | async-done | bytes 2359312
  333.4 0.9 constant_dynamic-slice_fusion
  334.3 0.7 copy_multiply_fusion
  (3 shorter events, 0.0 us)
Async XLA Ops:
  7.6 17.4 %collective-permute-start = (bf16[96,2048]{1,0:T(8,128)(2,1)S(1)}, bf16[96,2048]{1,0:T(8,128)(2,1)S(1)}, u32[]{:S(2)}, u32[]{:S(2)}) collective-permute-start(bf16[96,2048]{1,0:T(8,128)(2,1)S(1)} %slice.70), channel_id=1, source_target_pairs={{8,0},{16,8},{24,16},{32,24},{40,32},{48,40},{56,48},{64,56},{72,6... | collective-permute-start | bytes 1179656 | tf_op jit(solution)/shard_map/ppermute | solution.py:15
  24.1 1.4 copy-start
  38.9 13.8 %all-to-all-start = ((bf16[8,32,8,96]{3,1,2,0:T(8,128)(2,1)}), bf16[8,32,8,96]{3,1,2,0:T(8,128)(2,1)S(1)}, u32[]{:S(2)}, u32[]{:S(2)}) async-start(bf16[8,32,8,96]{3,1,2,0:T(8,128)(2,1)} %stack.8), calls=%async_computation | async-start | bytes 1048576 | tf_op jit(solution)/shard_map/all_to_all | solution.py:86
  42.4 290.9 %all-reduce.3.cloned.1.call-start = ((), (), s32[]{:S(2)}) async-start(), calls=%async_computation.1 | async-start | bytes 6291456
  58.0 0.7 copy-start.1
Sparse Core Ops, SparseCore 0:
  58.1 275.2 all-reduce.2
